TPU v7x, 256 devices: a whole 4x4x8 slice. The times are simulated.
256 devices in a mesh: state: 8 (over z), tile: 32 (over x, y, core).
Axes of the slice: x: 4, y: 4, z: 8, core: 2. Of those that a mesh axis runs over, the one named last changes fastest.
Arguments:
- bands: bfloat16 [8, 240, 524288], P('state', None, 'tile')
- block_slot: int32 [8, 4096], P('state', 'tile'), may hold values from 0 to 7
- tile_counties: int32 [8, 256], P('state', 'tile'), may hold values from 0 to 383, as said below
- county_place: int32 [8, 384], P('state'), may hold values from 0 to 383, as said below
- label: int32 [8, 384], P('state', 'tile'), may hold values from -200 to 200
- w_first: bfloat16 [64, 240], replicated, may hold values from -0.375 to 0.375
- taps: float32 [3, 64], replicated, may hold values from -2 to 2
- w_second: bfloat16 [128, 64], replicated, may hold values from -0.75 to 0.75
- w_third: bfloat16 [128, 128], replicated, may hold values from -0.5 to 0.5
- w_head: bfloat16 [128], replicated, may hold values from -0.5 to 0.5
Outputs:
- county_mean: float32 [8, 384], P('state', 'tile')
- weight_grads: float32 [40256], replicated
Inputs may be any that keep to these rules, and one draw needn't show every extreme that they name: `county_place`: each row is an ordering of the counties of one state region; the county at place p is owned by tile index p // 12 of that region. `tile_counties`: tile t's list names counties of its own state region owned by tile indices t, t + 1, ..., t + 4 - 1 (mod the tile axis's size); at most 4 entries of a list are owned by one tile index, and exactly 4 by t itself.
All inputs are finite; a program needn't handle non-finite values.
Results may differ from a plain program's by a relative error of at most 0.00064.
Values sent between devices are 32-bit elements; how exact they have to be, the bound alone decides.
No kernel may reach another device: no remote copies, remote signals or barrier semaphores. Data moves between devices by JAX's collectives and lax.ppermute only.
A program may use at most 128 MiB of HBM per device.

v0:
```python
import jax
import jax.numpy as jnp
from jax import lax
from jax.sharding import PartitionSpec as P

MOST = 4
REACH = 4


def from_behind(value, axis, by):
    peers = lax.axis_size(axis)
    return lax.ppermute(value, axis, [(i, (i + by) % peers) for i in range(peers)])


def silu_parts(value):
    sig = jax.nn.sigmoid(value)
    return (value * sig, sig * (1.0 + value * (1.0 - sig)))


def along_rows(field, weights, row_len):
    chans, count = field.shape
    grid = field.reshape(chans, count // row_len, row_len)
    padded = jnp.pad(grid, ((0, 0), (0, 0), (1, 1)))
    out = (
        weights[0][:, None, None] * padded[:, :, :-2]
        + weights[1][:, None, None] * grid
        + weights[2][:, None, None] * padded[:, :, 2:]
    )
    return out.reshape(chans, count)


def tap_grads(field, upstream, row_len):
    chans, count = field.shape
    grid = field.reshape(chans, count // row_len, row_len)
    padded = jnp.pad(grid, ((0, 0), (0, 0), (1, 1)))
    above = upstream.reshape(grid.shape)
    return jnp.stack(
        [
            jnp.sum(above * padded[:, :, :-2], axis=(1, 2)),
            jnp.sum(above * grid, axis=(1, 2)),
            jnp.sum(above * padded[:, :, 2:], axis=(1, 2)),
        ]
    )


def contract_last(left, right):
    return lax.dot_general(
        left, right, (((1,), (1,)), ((), ())), preferred_element_type=jnp.float32
    )


def contract_first(left, right):
    return lax.dot_general(
        left, right, (((0,), (0,)), ((), ())), preferred_element_type=jnp.float32
    )


def forward(pixels, w_first, taps, w_second, w_third, w_head, row_len):
    h_one = jnp.dot(w_first, pixels, preferred_element_type=jnp.float32)
    s_one = along_rows(h_one, taps, row_len)
    a_one = silu_parts(s_one)[0].astype(jnp.bfloat16)
    h_two = jnp.dot(w_second, a_one, preferred_element_type=jnp.float32)
    a_two = silu_parts(h_two)[0].astype(jnp.bfloat16)
    h_three = jnp.dot(w_third, a_two, preferred_element_type=jnp.float32)
    a_three = (silu_parts(h_three)[0] + a_two.astype(jnp.float32)).astype(jnp.bfloat16)
    yhat = jnp.dot(w_head, a_three, preferred_element_type=jnp.float32)
    return (h_one, s_one, a_one, h_two, a_two, h_three, a_three, yhat)


def backward(pixels, saved, taps, w_second, w_third, w_head, cotangent, row_len):
    h_one, s_one, a_one, h_two, a_two, h_three, a_three, yhat = saved
    grad_in = cotangent.astype(jnp.bfloat16)
    d_head = jnp.dot(a_three, grad_in, preferred_element_type=jnp.float32)
    d_a3 = w_head.astype(jnp.float32)[:, None] * grad_in.astype(jnp.float32)[None, :]
    d_h3 = (d_a3 * silu_parts(h_three)[1]).astype(jnp.bfloat16)
    d_third = contract_last(d_h3, a_two)
    d_a2 = contract_first(w_third, d_h3) + d_a3
    d_h2 = (d_a2 * silu_parts(h_two)[1]).astype(jnp.bfloat16)
    d_second = contract_last(d_h2, a_one)
    d_a1 = contract_first(w_second, d_h2)
    d_s1 = d_a1 * silu_parts(s_one)[1]
    d_taps = tap_grads(h_one, d_s1, row_len)
    d_h1 = along_rows(d_s1, jnp.stack([taps[2], taps[1], taps[0]]), row_len).astype(jnp.bfloat16)
    d_first = contract_last(d_h1, pixels)
    return jnp.concatenate(
        [d_first.reshape(-1), d_taps.reshape(-1), d_second.reshape(-1), d_third.reshape(-1), d_head]
    )


def slot_stats(yhat, slots, slot_count):
    blocks = slots.shape[0]
    row_len = yhat.shape[0] // blocks
    member = (slots[None, :] == jnp.arange(slot_count, dtype=jnp.int32)[:, None]).astype(
        jnp.float32
    )
    block_sums = jnp.sum(yhat.reshape(blocks, row_len), axis=1)
    return (
        jnp.sum(member * block_sums[None, :], axis=1),
        jnp.sum(member, axis=1) * row_len,
        member,
    )


def place_of(counties, table):
    hits = counties[:, None] == jnp.arange(table.shape[0], dtype=jnp.int32)[None, :]
    return jnp.sum(jnp.where(hits, table[None, :], 0), axis=1)


def judge(sums, counts, labels, devices):
    denom = jnp.maximum(counts, 1.0)
    mean = sums / denom
    live = (counts > 0.5).astype(jnp.float32)
    target = labels.astype(jnp.float32) * 0.01
    return (mean, live * 2.0 * (mean - target) / (devices * denom))


def pixel_cotangent(member, slot_adjoint, row_len):
    block_adjoint = jnp.sum(member * slot_adjoint[:, None], axis=0)
    return jnp.broadcast_to(block_adjoint[:, None], (block_adjoint.shape[0], row_len)).reshape(-1)


def settle(sums, counts, codes, labels, devices):
    flat_codes = codes.reshape(-1)
    owned = jnp.arange(1, labels.shape[0] + 1, dtype=jnp.int32).astype(jnp.float32)
    hit = (flat_codes[:, None] == owned[None, :]).astype(jnp.float32)
    total = jnp.sum(hit * sums.reshape(-1)[:, None], axis=0)
    number = jnp.sum(hit * counts.reshape(-1)[:, None], axis=0)
    mean, adjoint = judge(total, number, labels, devices)
    back = jnp.sum(hit * adjoint[None, :], axis=1).reshape(codes.shape)
    return (mean, back)


def packed(select, values, rows):
    return jnp.sum(select * values[:, None], axis=0).reshape(rows, -1)


def on_device(
    bands, block_slot, tile_counties, county_place, label, w_first, taps, w_second, w_third, w_head
):
    pixels = bands[0]
    slots = block_slot[0]
    row_len = pixels.shape[1] // slots.shape[0]
    slot_total = tile_counties.shape[1]
    saved = forward(pixels, w_first, taps, w_second, w_third, w_head, row_len)
    slot_sums, slot_counts, member = slot_stats(saved[-1], slots, slot_total)
    table = county_place[0]
    place = place_of(tile_counties[0], table)
    labels_mine = label[0]
    cty_dev = labels_mine.shape[0]
    n_tile = lax.axis_size("tile")
    devices = float(lax.axis_size("state") * n_tile)
    owner = place // cty_dev
    local_code = (place % cty_dev + 1).astype(jnp.float32)
    order = jnp.arange(slot_total, dtype=jnp.int32)
    rank = jnp.sum(
        ((owner[:, None] == owner[None, :]) & (order[None, :] < order[:, None])).astype(jnp.int32),
        axis=1,
    )
    me = lax.axis_index("tile")
    position = (owner - me) % n_tile * MOST + rank
    select = (position[:, None] == jnp.arange(REACH * MOST, dtype=jnp.int32)[None, :]).astype(
        jnp.float32
    )
    out_sums = packed(select, slot_sums, REACH)
    out_counts = packed(select, slot_counts, REACH)
    out_codes = packed(select, local_code, REACH)
    got_sums, got_counts, got_codes = ([], [], [])
    for step in range(REACH):
        if step == 0:
            piece = (out_sums[0], out_counts[0], out_codes[0])
        else:
            piece = from_behind((out_sums[step], out_counts[step], out_codes[step]), "tile", step)
        got_sums.append(piece[0])
        got_counts.append(piece[1])
        got_codes.append(piece[2])
    county_mean, back = settle(
        jnp.stack(got_sums), jnp.stack(got_counts), jnp.stack(got_codes), labels_mine, devices
    )
    rows = []
    for step in range(REACH):
        if step == 0:
            rows.append(back[0])
        else:
            rows.append(from_behind(back[step], "tile", -step))
    returned = jnp.stack(rows).reshape(-1)
    slot_adjoint = jnp.sum(select * returned[None, :], axis=1)
    cotangent = pixel_cotangent(member, slot_adjoint, row_len)
    local_grads = backward(pixels, saved, taps, w_second, w_third, w_head, cotangent, row_len)
    weight_grads = lax.psum(local_grads, ("state", "tile"))
    return (county_mean[None, :], weight_grads)


def solution(mesh):
    in_specs = (
        P("state", None, "tile"),
        P("state", "tile"),
        P("state", "tile"),
        P("state", None),
        P("state", "tile"),
        P(),
        P(),
        P(),
        P(),
        P(),
    )
    out_specs = (P("state", "tile"), P())
    return jax.shard_map(
        on_device, mesh=mesh, in_specs=in_specs, out_specs=out_specs, check_vma=False
    )
```

profile of v0, /device:TPU:1, one launch (start us, length us, event | category | flops | bytes accessed | tf_op | source)
XLA Modules:
  0.0 352.5 jit_solution(9751502985637400692)
XLA Ops:
  7.2 0.8 slice_bitcast_fusion.5
  8.0 4.7 %fusion.5 = f32[64,128,128]{2,0,1:T(8,128)S(1)} fusion(bf16[64,240]{1,0:T(8,128)(2,1)} %param.15, bf16[1,240,16384]{2,1,0:T(8,128)(2,1)} %param.10), kind=kOutput, calls=%fused_computation.18 | convolution fusion | flops 503316480 | bytes 12089344 | tf_op jit(solution)/shard_map/dot_general | solution.py:59
  12.8 2.4 fusion.18
  15.2 4.6 %multiply_convert_fusion = (bf16[128,16384]{0,1:T(8,128)(2,1)S(1)}, f32[128,16384]{0,1:T(8,128)}) fusion(bf16[64,16384]{1,0:T(8,128)(2,1)S(1)} %fusion.18, bf16[128,64]{0,1:T(8,128)(2,1)S(1)} %copy-done.12), kind=kOutput, calls=%fused_computation.16 | convolution fusion | flops 278921216 | bytes 14696448 | tf_op jit(solution)/shard_map/dot_general | solution.py:62
  19.8 4.6 %add_convert_fusion = (bf16[128,16384]{0,1:T(8,128)(2,1)S(1)}, f32[128,16384]{0,1:T(8,128)}) fusion(bf16[128,16384]{0,1:T(8,128)(2,1)S(1)} %get-tuple-element.37, bf16[128,128]{1,0:T(8,128)(2,1)S(1)} %copy-done), kind=kOutput, calls=%fused_computation.14 | convolution fusion | flops 551550976 | bytes 16809984 | tf_op jit(solution)/shard_map/dot_general | solution.py:64
  24.5 1.9 copy-done.3
  26.5 1.2 fusion.38
  27.6 0.1 reduce_sum.147
  27.8 0.1 convert_reduce_fusion
  28.0 0.2 select_reduce_fusion
  28.2 0.2 convert_reduce_fusion.1
  28.5 2.7 collective-permute-start.3
  31.2 1.3 collective-permute-start.4
  32.5 1.7 collective-permute-start.5
  34.3 0.5 collective-permute-start
  34.7 1.3 collective-permute-start.1
  36.1 2.1 collective-permute-start.2
  38.3 0.5 collective-permute-start.6
  38.7 0.1 collective-permute-done.5
  38.8 0.8 collective-permute-start.7
  39.7 2.2 collective-permute-start.8
  41.9 0.6 collective-permute-done.2
  42.6 2.0 collective-permute-done.7
  44.6 1.5 collective-permute-done.8
  46.1 0.1 fusion.27
  46.2 0.5 fusion.40
  46.8 0.2 fusion.28
  47.0 0.9 collective-permute-start.9
  47.9 2.0 collective-permute-start.10
  49.9 0.3 collective-permute-start.11
  50.2 0.4 collective-permute-done.10
  50.6 3.8 %collective-permute-done.11 = f32[4]{0:T(128)S(1)} collective-permute-done((f32[4]{0:T(128)S(1)}, f32[4]{0:T(128)S(1)}, u32[]{:S(2)}, u32[]{:S(2)}) %collective-permute-start.11) | collective-permute-done | bytes 48 | tf_op jit(solution)/shard_map/ppermute | solution.py:12
  54.5 0.2 select_reduce_fusion.2
  54.9 10.0 %fusion.4 = bf16[128,16384]{0,1:T(8,128)(2,1)S(1)} fusion(f32[128,16384]{0,1:T(8,128)} %get-tuple-element.40, f32[16384]{0:T(1024)S(1)} %get-tuple-element.18, f32[128]{0:T(128)S(1)} %convert_element_type.84), kind=kLoop, calls=%fused_computation.13 | loop fusion | flops 20971520 | bytes 12648960 | tf_op jit(solution)/shard_map/convert_element_type | solution.py:75
  64.9 1.4 convolution_bitcast_fusion.4
  66.3 0.8 slice-done.1
  67.1 7.6 %fusion.2 = bf16[128,16384]{0,1:T(8,128)(2,1)S(1)} fusion(bf16[128,16384]{0,1:T(8,128)(2,1)S(1)} %fusion.4, bf16[128,128]{1,0:T(8,128)(2,1)S(1)} %copy-done, f32[128,16384]{0,1:T(8,128)S(1)} %bitcast.178, f32[16384]{0:T(1024)S(1)} %get-tuple-element.18, f32[128]{0:T(128)S(1)} %convert_element_type.84), kind=kOutput, calls=%fused_computation.5 | convolution fusion | flops 559939584 | bytes 16876032 | tf_op jit(solution)/shard_map/dot_general | solution.py:53
  74.7 3.5 fusion.21
  78.1 2.5 multiply_reduce_fusion.2
  80.6 2.5 copy.55
  83.1 1.3 fusion.41
  84.5 0.8 copy-done.4
  85.3 0.7 convolution_bitcast_fusion.5
  86.1 9.2 %fusion.8 = f32[64,240]{1,0:T(8,128)S(1)} fusion(bf16[1,240,16384]{2,1,0:T(8,128)(2,1)} %param.10, f32[64,128,128]{2,0,1:T(8,128)} %bitcast.157, f32[64]{0:T(128)S(1)} %get-tuple-element.14, f32[64]{0:T(128)S(1)} %get-tuple-element.16, f32[64]{0:T(128)S(1)} %get-tuple-element.15), kind=kOutput, calls=%fused_computation.21 | convolution fusion | flops 509607936 | bytes 12120832 | tf_op jit(solution)/shard_map/dot_general | solution.py:47
  95.3 0.1 reshape.182
  95.5 0.8 concatenate.3
  96.3 247.7 %all-reduce.4.cloned.1.call-done = f32[40256]{0:T(1024)} async-done(((f32[40256]{0:T(1024)}), f32[40256]{0:T(1024)}) %all-reduce.4.cloned.1.call-update) | async-done | bytes 161040 | tf_op jit(solution)/shard_map/psum | solution.py:189
  344.0 1.6 copy.57
  (61 shorter events, 1.3 us)
Async XLA Ops:
  7.2 12.7 %copy-start = (bf16[128,128]{1,0:T(8,128)(2,1)S(1)}, bf16[128,128]{1,0:T(8,128)(2,1)}, u32[]{:S(2)}) copy-start(bf16[128,128]{1,0:T(8,128)(2,1)} %param.18) | copy-start | bytes 98308
  7.2 336.8 %all-reduce.4.cloned.1.call-start = ((), (), s32[]{:S(2)}) async-start(), calls=%async_computation | async-start | bytes 327680 | tf_op jit(solution)/shard_map/psum | solution.py:189
  12.8 7.1 %copy-start.1 = (f32[64,128,128]{2,0,1:T(8,128)}, f32[64,128,128]{2,0,1:T(8,128)S(1)}, u32[]{:S(2)}) copy-start(f32[64,128,128]{2,0,1:T(8,128)S(1)} %fusion.5) | copy-start | bytes 12582916
  12.8 2.4 copy-start.12
  19.8 4.6 %copy-start.5 = (bf16[128,16384]{0,1:T(8,128)(2,1)}, bf16[128,16384]{0,1:T(8,128)(2,1)S(1)}, u32[]{:S(2)}) copy-start(bf16[128,16384]{0,1:T(8,128)(2,1)S(1)} %get-tuple-element.37) | copy-start | bytes 12582916
  19.8 6.6 %copy-start.8 = (bf16[128]{0:T(256)(128)(2,1)S(1)}, bf16[128]{0:T(256)(128)(2,1)}, u32[]{:S(2)}) copy-start(bf16[128]{0:T(256)(128)(2,1)} %param.19) | copy-start | bytes 772
  24.5 2.0 copy-start.3
  24.5 3.3 copy-start.11
  24.5 3.4 copy-start.7
  24.5 3.5 copy-start.10
  24.5 21.7 %copy-start.9 = (s32[1,12]{1,0:T(1,128)S(1)}, s32[1,12]{1,0:T(1,128)}, u32[]{:S(2)}) copy-start(s32[1,12]{1,0:T(1,128)} %param.14) | copy-start | bytes 148
  28.5 7.6 %collective-permute-start.3 = (f32[4]{0:T(128)S(1)}, f32[4]{0:T(128)S(1)}, u32[]{:S(2)}, u32[]{:S(2)}) collective-permute-start(f32[4]{0:T(128)S(1)} %get-tuple-element.26), channel_id=1, source_target_pairs={{0,1},{1,2},{2,3},{3,4},{4,5},{5,6},{6,7},{7,8},{8,9},{9,10},{10,1... | collective-permute-start | bytes 56 | tf_op jit(solution)/shard_map/ppermute | solution.py:12
  31.2 7.0 %collective-permute-start.4 = (f32[4]{0:T(128)S(1)}, f32[4]{0:T(128)S(1)}, u32[]{:S(2)}, u32[]{:S(2)}) collective-permute-start(f32[4]{0:T(128)S(1)} %get-tuple-element.25), channel_id=1, source_target_pairs={{0,2},{1,3},{2,4},{3,5},{4,6},{5,7},{6,8},{7,9},{8,10},{9,11},{10,... | collective-permute-start | bytes 56 | tf_op jit(solution)/shard_map/ppermute | solution.py:12
  32.5 6.3 %collective-permute-start.5 = (f32[4]{0:T(128)S(1)}, f32[4]{0:T(128)S(1)}, u32[]{:S(2)}, u32[]{:S(2)}) collective-permute-start(f32[4]{0:T(128)S(1)} %get-tuple-element.24), channel_id=1, source_target_pairs={{0,3},{1,4},{2,5},{3,6},{4,7},{5,8},{6,9},{7,10},{8,11},{9,12},{10... | collective-permute-start | bytes 56 | tf_op jit(solution)/shard_map/ppermute | solution.py:12
  34.3 5.4 %collective-permute-start = (f32[4]{0:T(128)S(1)}, f32[4]{0:T(128)S(1)}, u32[]{:S(2)}, u32[]{:S(2)}) collective-permute-start(f32[4]{0:T(128)S(1)} %get-tuple-element.30), channel_id=1, source_target_pairs={{0,1},{1,2},{2,3},{3,4},{4,5},{5,6},{6,7},{7,8},{8,9},{9,10},{10,1... | collective-permute-start | bytes 56 | tf_op jit(solution)/shard_map/ppermute | solution.py:12
  34.7 7.1 %collective-permute-start.1 = (f32[4]{0:T(128)S(1)}, f32[4]{0:T(128)S(1)}, u32[]{:S(2)}, u32[]{:S(2)}) collective-permute-start(f32[4]{0:T(128)S(1)} %get-tuple-element.29), channel_id=1, source_target_pairs={{0,2},{1,3},{2,4},{3,5},{4,6},{5,7},{6,8},{7,9},{8,10},{9,11},{10,... | collective-permute-start | bytes 56 | tf_op jit(solution)/shard_map/ppermute | solution.py:12
  36.1 6.3 %collective-permute-start.2 = (f32[4]{0:T(128)S(1)}, f32[4]{0:T(128)S(1)}, u32[]{:S(2)}, u32[]{:S(2)}) collective-permute-start(f32[4]{0:T(128)S(1)} %get-tuple-element.28), channel_id=1, source_target_pairs={{0,3},{1,4},{2,5},{3,6},{4,7},{5,8},{6,9},{7,10},{8,11},{9,12},{10... | collective-permute-start | bytes 56 | tf_op jit(solution)/shard_map/ppermute | solution.py:12
  38.3 4.3 %collective-permute-start.6 = (f32[4]{0:T(128)S(1)}, f32[4]{0:T(128)S(1)}, u32[]{:S(2)}, u32[]{:S(2)}) collective-permute-start(f32[4]{0:T(128)S(1)} %get-tuple-element.34), channel_id=1, source_target_pairs={{0,1},{1,2},{2,3},{3,4},{4,5},{5,6},{6,7},{7,8},{8,9},{9,10},{10,1... | collective-permute-start | bytes 56 | tf_op jit(solution)/shard_map/ppermute | solution.py:12
  38.8 5.7 %collective-permute-start.7 = (f32[4]{0:T(128)S(1)}, f32[4]{0:T(128)S(1)}, u32[]{:S(2)}, u32[]{:S(2)}) collective-permute-start(f32[4]{0:T(128)S(1)} %get-tuple-element.33), channel_id=1, source_target_pairs={{0,2},{1,3},{2,4},{3,5},{4,6},{5,7},{6,8},{7,9},{8,10},{9,11},{10,... | collective-permute-start | bytes 56 | tf_op jit(solution)/shard_map/ppermute | solution.py:12
  39.7 6.3 %collective-permute-start.8 = (f32[4]{0:T(128)S(1)}, f32[4]{0:T(128)S(1)}, u32[]{:S(2)}, u32[]{:S(2)}) collective-permute-start(f32[4]{0:T(128)S(1)} %get-tuple-element.32), channel_id=1, source_target_pairs={{0,3},{1,4},{2,5},{3,6},{4,7},{5,8},{6,9},{7,10},{8,11},{9,12},{10... | collective-permute-start | bytes 56 | tf_op jit(solution)/shard_map/ppermute | solution.py:12
  47.0 3.2 collective-permute-start.9
  47.9 2.7 collective-permute-start.10
  49.9 4.5 %collective-permute-start.11 = (f32[4]{0:T(128)S(1)}, f32[4]{0:T(128)S(1)}, u32[]{:S(2)}, u32[]{:S(2)}) collective-permute-start(f32[4]{0:T(128)S(1)} %get-tuple-element.20), channel_id=1, source_target_pairs={{0,29},{1,30},{2,31},{3,0},{4,1},{5,2},{6,3},{7,4},{8,5},{9,6},{10... | collective-permute-start | bytes 56 | tf_op jit(solution)/shard_map/ppermute | solution.py:12
  54.9 10.0 %copy-start.6 = (bf16[128,16384]{0,1:T(8,128)(2,1)S(1)}, bf16[128,16384]{0,1:T(8,128)(2,1)}, u32[]{:S(2)}) copy-start(bf16[128,16384]{0,1:T(8,128)(2,1)} %copy-done.5) | copy-start | bytes 12582916
  54.9 11.4 %slice-start = ((s8[8388608]{0:T(1024)(128)(4,1)}), s8[4194304]{0:T(1024)(128)(4,1)S(1)}, s32[]{:S(2)}) async-start(s8[8388608]{0:T(1024)(128)(4,1)} %bitcast.177), calls=%async_computation.1 | async-start | bytes 8388608
  64.9 2.2 slice-start.1
  67.1 7.6 %copy-start.2 = (f32[64,128,128]{2,0,1:T(8,128)S(1)}, f32[64,128,128]{2,0,1:T(8,128)}, u32[]{:S(2)}) copy-start(f32[64,128,128]{2,0,1:T(8,128)} %copy-done.1) | copy-start | bytes 12582916
  83.1 2.2 copy-start.4
Sparse Core Ops, SparseCore 0:
  96.5 247.5 all-reduce.3
where the time goes:
time: 353 us; the launch traced here: 352 us
  waiting for transfers between devices  256 us (73%)
  matrix products  38.8 us (11%)
  other arithmetic  16.9 us (5%)
  starting transfers between devices  16.2 us (5%)
  between operations  14.3 us (4%)
  local copies, waits for them, and re-layouts  10.2 us (3%)
    psum x1, waiting for transfers between devices, on_device(): weight_grads = lax.psum(local_grads, ('state', 'tile'))  248 us
    ppermute x12, starting transfers between devices, from_behind(): lax.ppermute(value, axis, [(i, (i + by) % peers) for i in range(peers)])  16.2 us
    dot_general x3, matrix products, contract_last(): lax.dot_general(left, right, (((1,), (1,)), ((), ())), preferred_element_...  12 us
    dot_general x2, matrix products, contract_first(): lax.dot_general(left, right, (((0,), (0,)), ((), ())), preferred_element_...  11 us
    convert_element_type x1, other arithmetic, backward(): d_h3 = (d_a3 * silu_parts(h_three)[1]).astype(jnp.bfloat16)  9.98 us
    ppermute x12, waiting for transfers between devices, from_behind(): lax.ppermute(value, axis, [(i, (i + by) % peers) for i in range(peers)])  8.37 us
  transfers between devices with their start and end apart: 13, of which 7 were waited for; matrix products, arithmetic and copies ran while one was open for 0% of the time, Pallas kernels for 0%

commit v1 on v0

--- a/solution.py
+++ b/solution.py
@@ -5,6 +5,12 @@
 
 MOST = 4
 REACH = 4
+
+
+def gather_and_add(block, name):
+    parts = lax.all_gather(block, name, axis=0, tiled=False)
+    total = parts.sum(axis=0)
+    return total
 
 
 def from_behind(value, axis, by):
@@ -186,7 +192,7 @@
     slot_adjoint = jnp.sum(select * returned[None, :], axis=1)
     cotangent = pixel_cotangent(member, slot_adjoint, row_len)
     local_grads = backward(pixels, saved, taps, w_second, w_third, w_head, cotangent, row_len)
-    weight_grads = lax.psum(local_grads, ("state", "tile"))
+    weight_grads = gather_and_add(local_grads, ("state", "tile"))
     return (county_mean[None, :], weight_grads)
 
 

time: 353 us -> 608 us (1.72)
  waiting for transfers between devices: 256 us -> 441 us
  local copies, waits for them, and re-layouts: 10.2 us -> 59.9 us
  other arithmetic: 16.9 us -> 33.7 us
    unnamed x1 -> x2, waiting for transfers between devices: 0.02 us -> 435 us
    psum x1 -> x0, waiting for transfers between devices: 248 us -> none  [on_device(): weight_grads = lax.psum(local_grads, ('state', 'tile'))]
    all_gather x0 -> x1, local copies, waits for them, and re-layouts: none -> 36.1 us  [gather_and_add(): parts = lax.all_gather(block, name, axis=0, tiled=False)]
    reduce_sum x0 -> x1, other arithmetic: none -> 15.5 us  [gather_and_add(): total = parts.sum(axis=0)]
    unnamed x31 -> x28, local copies, waits for them, and re-layouts: 5.17 us -> 19.4 us
where the time goes in v1:
time: 608 us; the launch traced here: 606 us
  waiting for transfers between devices  441 us (73%)
  local copies, waits for them, and re-layouts  59.9 us (10%)
  matrix products  40.9 us (7%)
  other arithmetic  33.7 us (6%)
  starting transfers between devices  16.1 us (3%)
  between operations  14.3 us (2%)
    unnamed x2, waiting for transfers between devices  435 us
    all_gather x1, local copies, waits for them, and re-layouts, gather_and_add(): parts = lax.all_gather(block, name, axis=0, tiled=False)  36.1 us
    unnamed x28, local copies, waits for them, and re-layouts  19.4 us
    ppermute x12, starting transfers between devices, from_behind(): lax.ppermute(value, axis, [(i, (i + by) % peers) for i in range(peers)])  16.1 us
    reduce_sum x1, other arithmetic, gather_and_add(): total = parts.sum(axis=0)  15.5 us
  transfers between devices with their start and end apart: 13, of which 7 were waited for; matrix products, arithmetic and copies ran while one was open for 0% of the time, Pallas kernels for 0%

profile of v1, /device:TPU:1, one launch (start us, length us, event | category | flops | bytes accessed | tf_op | source)
XLA Modules:
  0.0 606.4 jit_solution(5181082057389946123)
XLA Ops:
  7.2 0.8 slice_bitcast_fusion.5
  8.0 0.7 reduce
  8.7 0.8 select_reduce_fusion
  9.6 0.2 convert_reduce_fusion.1
  9.8 4.8 fusion.5
  14.5 2.4 fusion.18
  17.0 4.6 multiply_convert_fusion
  21.6 4.6 add_convert_fusion
  26.2 2.0 copy-done.4
  28.2 1.2 fusion.38
  29.5 0.1 convert_reduce_fusion
  29.8 4.3 collective-permute-start.2
  34.2 0.4 collective-permute-start.1
  34.6 0.3 collective-permute-start
  34.9 2.6 collective-permute-start.5
  37.5 1.3 collective-permute-start.4
  38.9 0.5 collective-permute-start.3
  39.4 0.5 collective-permute-done.1
  39.9 0.6 collective-permute-start.8
  40.5 1.7 collective-permute-start.7
  42.3 0.6 collective-permute-start.6
  42.9 0.4 collective-permute-done.4
  43.4 2.9 collective-permute-done.8
  46.4 0.5 fusion.40
  46.9 0.2 fusion.28
  47.2 2.4 collective-permute-start.11
  49.6 1.2 collective-permute-start.10
  50.8 0.2 collective-permute-start.9
  51.0 0.7 collective-permute-done.11
  51.7 0.4 collective-permute-done.10
  52.1 1.7 collective-permute-done.9
  53.9 0.2 select_reduce_fusion.2
  54.3 10.0 %fusion.4 = bf16[128,16384]{0,1:T(8,128)(2,1)S(1)} fusion(f32[128,16384]{0,1:T(8,128)} %get-tuple-element.40, f32[16384]{0:T(1024)S(1)} %get-tuple-element.18, f32[128]{0:T(128)S(1)} %convert_element_type.84), kind=kLoop, calls=%fused_computation.13 | loop fusion | flops 20971520 | bytes 12648960 | tf_op jit(solution)/shard_map/convert_element_type | solution.py:81
  64.3 1.4 convolution_bitcast_fusion.4
  65.7 0.8 slice-done.1
  66.5 7.5 %fusion.2 = bf16[128,16384]{0,1:T(8,128)(2,1)S(1)} fusion(bf16[128,16384]{0,1:T(8,128)(2,1)S(1)} %fusion.4, bf16[128,128]{1,0:T(8,128)(2,1)S(1)} %copy-done, f32[128,16384]{0,1:T(8,128)S(1)} %bitcast.178, f32[16384]{0:T(1024)S(1)} %get-tuple-element.18, f32[128]{0:T(128)S(1)} %convert_element_type.84), kind=kOutput, calls=%fused_computation.5 | convolution fusion | flops 559939584 | bytes 16876032 | tf_op jit(solution)/shard_map/dot_general | solution.py:59
  74.0 1.3 fusion.41
  75.4 0.9 copy-done.3
  76.2 3.4 fusion.21
  79.7 2.5 multiply_reduce_fusion.2
  82.1 2.5 copy.55
  84.7 9.2 %fusion.8 = f32[64,240]{1,0:T(8,128)S(1)} fusion(bf16[1,240,16384]{2,1,0:T(8,128)(2,1)} %param.10, f32[64,128,128]{2,0,1:T(8,128)} %bitcast.157, f32[64]{0:T(128)S(1)} %get-tuple-element.14, f32[64]{0:T(128)S(1)} %get-tuple-element.16, f32[64]{0:T(128)S(1)} %get-tuple-element.15), kind=kOutput, calls=%fused_computation.21 | convolution fusion | flops 509607936 | bytes 12120832 | tf_op jit(solution)/shard_map/dot_general | solution.py:53
  94.3 2.8 convolution_bitcast_fusion.5
  97.2 13.3 %broadcast.244 = f32[10305536]{0:T(1024)} broadcast(f32[]{:T(128)} %constant.60.clone.1), dimensions={} | broadcast | bytes 41222148
  110.5 2.5 dynamic-update-slice
  113.1 434.9 %all-reduce.5.cloned.1.call-done = f32[10305536]{0:T(1024)} async-done(((f32[10305536]{0:T(1024)}), f32[10305536]{0:T(1024)}) %all-reduce.5.cloned.1.call-update) | async-done | bytes 41222160
  548.0 36.1 %reshape.186 = f32[256,40256]{1,0:T(8,128)} reshape(f32[10305536]{0:T(1024)} %all-reduce.5.cloned.1.call-done) | data formatting | bytes 82444288 | tf_op jit(solution)/shard_map/all_gather | solution.py:11
  584.0 15.5 %reduce_sum.169 = f32[40256]{0:T(1024)} reduce(f32[256,40256]{1,0:T(8,128)} %reshape.186, f32[]{:T(128)} %constant.60.clone.1), dimensions={0}, to_apply=%region_16.17 | reduce | flops 10265280 | bytes 41383172 | tf_op jit(solution)/shard_map/reduce_sum | solution.py:12
  (60 shorter events, 1.7 us)
Async XLA Ops:
  7.2 14.4 %copy-start = (bf16[128,128]{1,0:T(8,128)(2,1)S(1)}, bf16[128,128]{1,0:T(8,128)(2,1)}, u32[]{:S(2)}) copy-start(bf16[128,128]{1,0:T(8,128)(2,1)} %param.18) | copy-start | bytes 98308
  7.2 540.8 %all-reduce.5.cloned.1.call-start = ((), (), s32[]{:S(2)}) async-start(), calls=%async_computation | async-start | bytes 82444288
  14.5 7.1 %copy-start.2 = (f32[64,128,128]{2,0,1:T(8,128)}, f32[64,128,128]{2,0,1:T(8,128)S(1)}, u32[]{:S(2)}) copy-start(f32[64,128,128]{2,0,1:T(8,128)S(1)} %fusion.5) | copy-start | bytes 12582916
  14.5 2.4 copy-start.10
  21.6 4.6 copy-start.5
  21.6 6.6 %copy-start.7 = (bf16[128]{0:T(256)(128)(2,1)S(1)}, bf16[128]{0:T(256)(128)(2,1)}, u32[]{:S(2)}) copy-start(bf16[128]{0:T(256)(128)(2,1)} %param.19) | copy-start | bytes 772
  26.2 2.0 copy-start.4
  26.2 3.3 copy-start.9
  26.2 20.2 %copy-start.8 = (s32[1,12]{1,0:T(1,128)S(1)}, s32[1,12]{1,0:T(1,128)}, u32[]{:S(2)}) copy-start(s32[1,12]{1,0:T(1,128)} %param.14) | copy-start | bytes 148
  29.8 9.1 %collective-permute-start.2 = (f32[4]{0:T(128)S(1)}, f32[4]{0:T(128)S(1)}, u32[]{:S(2)}, u32[]{:S(2)}) collective-permute-start(f32[4]{0:T(128)S(1)} %get-tuple-element.28), channel_id=1, source_target_pairs={{0,3},{1,4},{2,5},{3,6},{4,7},{5,8},{6,9},{7,10},{8,11},{9,12},{10... | collective-permute-start | bytes 56 | tf_op jit(solution)/shard_map/ppermute | solution.py:18
  34.2 5.7 collective-permute-start.1
  34.6 5.9 collective-permute-start
  34.9 7.4 %collective-permute-start.5 = (f32[4]{0:T(128)S(1)}, f32[4]{0:T(128)S(1)}, u32[]{:S(2)}, u32[]{:S(2)}) collective-permute-start(f32[4]{0:T(128)S(1)} %get-tuple-element.24), channel_id=1, source_target_pairs={{0,3},{1,4},{2,5},{3,6},{4,7},{5,8},{6,9},{7,10},{8,11},{9,12},{10... | collective-permute-start | bytes 56 | tf_op jit(solution)/shard_map/ppermute | solution.py:18
  37.5 5.7 collective-permute-start.4
  38.9 4.4 collective-permute-start.3
  39.9 6.3 %collective-permute-start.8 = (f32[4]{0:T(128)S(1)}, f32[4]{0:T(128)S(1)}, u32[]{:S(2)}, u32[]{:S(2)}) collective-permute-start(f32[4]{0:T(128)S(1)} %get-tuple-element.32), channel_id=1, source_target_pairs={{0,3},{1,4},{2,5},{3,6},{4,7},{5,8},{6,9},{7,10},{8,11},{9,12},{10... | collective-permute-start | bytes 56 | tf_op jit(solution)/shard_map/ppermute | solution.py:18
  40.5 5.7 collective-permute-start.7
  42.3 3.9 collective-permute-start.6
  47.2 4.5 collective-permute-start.11
  49.6 2.4 collective-permute-start.10
  50.8 3.0 collective-permute-start.9
  54.3 10.0 %copy-start.6 = (bf16[128,16384]{0,1:T(8,128)(2,1)S(1)}, bf16[128,16384]{0,1:T(8,128)(2,1)}, u32[]{:S(2)}) copy-start(bf16[128,16384]{0,1:T(8,128)(2,1)} %copy-done.5) | copy-start | bytes 12582916
  54.3 11.4 %slice-start = ((s8[8388608]{0:T(1024)(128)(4,1)}), s8[4194304]{0:T(1024)(128)(4,1)S(1)}, s32[]{:S(2)}) async-start(s8[8388608]{0:T(1024)(128)(4,1)} %bitcast.177), calls=%async_computation.1 | async-start | bytes 8388608
  64.3 2.2 slice-start.1
  74.0 2.2 copy-start.3
  584.0 15.5 %copy-start.1 = (bf16[128,128]{1,0:T(8,128)(2,1)S(1)}, bf16[128,128]{1,0:T(8,128)(2,1)}, u32[]{:S(2)}) copy-start(bf16[128,128]{1,0:T(8,128)(2,1)} %param.18) | copy-start | bytes 98308
Sparse Core Ops, SparseCore 0:
  113.2 434.7 all-reduce.4
